TPU v7x, 32 devices: a whole 2x2x4 slice. The times are simulated.
32 devices in a mesh: leaf: 16 (over z, y, x), col: 2 (over core).
Axes of the slice: x: 2, y: 2, z: 4, core: 2. Of those that a mesh axis runs over, the one named last changes fastest.
Arguments:
- sources: bfloat16 [65536, 256], P('leaf', 'col'), may hold values from -6 to 6
- near_tiles: bfloat16 [256, 8, 256, 256], P('leaf', 'col'), may hold values from -0.125 to 0.125
- near_index: int32 [256, 8], P('leaf'), may hold values from 0 to 255, as said below
- near_count: int32 [256], P('leaf'), may hold values from 1 to 8, as said below
- leaf_basis: bfloat16 [256, 64, 256], P('leaf'), may hold values from -0.375 to 0.375
- leaf_coupling: bfloat16 [256, 64, 256], P('leaf'), may hold values from -0.375 to 0.375
- leaf_far: int32 [256, 4], P('leaf'), may hold values from 0 to 255, as said below
- up_leaf: bfloat16 [32, 64, 512], P('leaf'), may hold values from -0.25 to 0.25
- mid_coupling: bfloat16 [32, 64, 256], P('leaf'), may hold values from -0.375 to 0.375
- mid_far: int32 [32, 4], P('leaf'), may hold values from 0 to 31, as said below
- up_mid: bfloat16 [32, 64, 64], P('leaf'), may hold values from -0.75 to 0.75
- top_coupling: bfloat16 [4, 64, 256], replicated, may hold values from -0.4375 to 0.4375
Outputs:
- product: float32 [65536, 256], P('leaf', 'col')
Inputs may be any that keep to these rules, and one draw needn't show every extreme that they name: `near_index`: entry 0 of row i is i; the other 7 entries are distinct leaves j with j != i and |i - j| <= 8. Only the first near_count[i] slots of leaf i count; some leaf has all 8. `leaf_far`: row i holds 4 distinct leaves j != i with |i // 8 - j // 8| <= 1. `mid_far`: row a holds 4 distinct middle clusters b != a with |a // 8 - b // 8| <= 1.
All inputs are finite; a program needn't handle non-finite values.
Results may differ from a plain program's by a relative error of at most 0.01.
Values may be sent and summed in bfloat16 or wider, within the bound.
No kernel may reach another device: no remote copies, remote signals or barrier semaphores. Data moves between devices by JAX's collectives and lax.ppermute only.
A program may use at most 128 MiB of HBM per device.

v0:
```python
import jax
import jax.numpy as jnp
from jax import lax
from jax.sharding import PartitionSpec as P

CHILD = 8
FAR = 4


def padded(x, sides, width):
    for axis, dim in sides:
        size, length = (lax.axis_size(axis), x.shape[dim])
        up = [(i, (i + 1) % size) for i in range(size - 1)]
        down = [(j, i) for i, j in up]
        last = lax.slice_in_dim(x, length - width, length, axis=dim)
        first = lax.slice_in_dim(x, 0, width, axis=dim)
        before = lax.ppermute(last, axis, up)
        after = lax.ppermute(first, axis, down)
        x = jnp.concatenate([before, x, after], axis=dim)
    return x


def shards(
    sources,
    near_tiles,
    near_index,
    near_count,
    leaf_basis,
    leaf_coupling,
    leaf_far,
    up_leaf,
    mid_coupling,
    mid_far,
    up_mid,
    top_coupling,
):
    f32 = jnp.float32
    bf16 = jnp.bfloat16
    leaf_count = leaf_basis.shape[0]
    rank_size = leaf_basis.shape[1]
    leaf_size = leaf_basis.shape[2]
    col_count = sources.shape[1]
    mid_count = leaf_count // CHILD
    total_top = top_coupling.shape[0]
    device = lax.axis_index("leaf")
    first_leaf = device * leaf_count
    first_mid = device * mid_count
    window = padded(sources, (("leaf", 0),), CHILD * leaf_size)
    near_local = near_index - (first_leaf - CHILD)
    all_tiles = lax.all_gather(near_tiles, "col", axis=1, tiled=True)
    slot_count = all_tiles.shape[1]
    blocks = window.reshape(-1, leaf_size, window.shape[1])
    picked = blocks[near_local]
    live_mask = jnp.arange(slot_count)[None, :] < near_count[:, None]
    picked = jnp.where(live_mask[:, :, None, None], picked, jnp.zeros((), bf16))
    result = jnp.einsum("lsij,lsjc->lic", all_tiles, picked, preferred_element_type=f32)
    near_part = result.reshape(leaf_count * leaf_size, window.shape[1])
    leaf_blocks = sources.reshape(leaf_count, leaf_size, col_count)
    leaf_coef = jnp.einsum(
        "lrk,lkc->lrc", leaf_basis, leaf_blocks, preferred_element_type=f32
    ).astype(bf16)
    mid_coef = jnp.einsum(
        "qrk,qkc->qrc",
        up_leaf,
        leaf_coef.reshape(mid_count, CHILD * rank_size, col_count),
        preferred_element_type=f32,
    ).astype(bf16)
    mid_lift = jnp.einsum("qrs,qsc->qrc", up_mid, mid_coef, preferred_element_type=f32).astype(bf16)
    parent = (first_mid + jnp.arange(mid_count)) // CHILD
    mid_flat = mid_far.reshape(-1)
    top_range = jnp.arange(total_top)
    coef_piece = lax.all_gather(mid_coef, "leaf", axis=0, tiled=True)
    lift_piece = lax.all_gather(mid_lift, "leaf", axis=0, tiled=True)
    global_ids = jnp.arange(coef_piece.shape[0])
    group_map = (top_range[:, None] == (global_ids // CHILD)[None, :]).astype(bf16)
    top_total = jnp.einsum("pk,krc->prc", group_map, lift_piece, preferred_element_type=f32)
    global_ids = jnp.arange(coef_piece.shape[0])
    pick_map = (mid_flat[:, None] == global_ids[None, :]).astype(bf16)
    mid_picked = jnp.einsum("ik,krc->irc", pick_map, coef_piece, preferred_element_type=f32)
    top_coef = top_total.astype(bf16)
    parent_rows = top_coupling[parent]
    keep_mask = top_range[None, :] != parent[:, None]
    stacked = jnp.where(keep_mask[:, :, None, None], top_coef[None], jnp.zeros((), bf16))
    top_field = jnp.einsum(
        "qrk,qkc->qrc",
        parent_rows,
        stacked.reshape(mid_count, total_top * rank_size, col_count),
        preferred_element_type=f32,
    ).astype(bf16)
    mid_chosen = mid_picked.astype(bf16).reshape(mid_count, FAR * rank_size, col_count)
    mid_field = (
        jnp.einsum("qrk,qkc->qrc", mid_coupling, mid_chosen, preferred_element_type=f32)
        + jnp.einsum("qrs,qrc->qsc", up_mid, top_field, preferred_element_type=f32)
    ).astype(bf16)
    leaf_window = padded(leaf_coef, (("leaf", 0),), CHILD)
    far_local = leaf_far - (first_leaf - CHILD)
    leaf_chosen = leaf_window[far_local].reshape(leaf_count, FAR * rank_size, col_count)
    down_part = jnp.einsum("qrs,qrc->qsc", up_leaf, mid_field, preferred_element_type=f32).reshape(
        leaf_count, rank_size, col_count
    )
    leaf_field = (
        jnp.einsum("lrk,lkc->lrc", leaf_coupling, leaf_chosen, preferred_element_type=f32)
        + down_part
    ).astype(bf16)
    far_part = jnp.einsum(
        "lrk,lrc->lkc", leaf_basis, leaf_field, preferred_element_type=f32
    ).reshape(leaf_count * leaf_size, col_count)
    return near_part + far_part


def solution(mesh):
    return jax.shard_map(
        shards,
        mesh=mesh,
        in_specs=(
            P("leaf", "col"),
            P("leaf", "col", None, None),
            P("leaf", None),
            P("leaf"),
            P("leaf", None, None),
            P("leaf", None, None),
            P("leaf", None),
            P("leaf", None, None),
            P("leaf", None, None),
            P("leaf", None),
            P("leaf", None, None),
            P(),
        ),
        out_specs=P("leaf", "col"),
        check_vma=False,
    )
```

profile of v0, /device:TPU:0, one launch (start us, length us, event | category | flops | bytes accessed | tf_op | source)
XLA Modules:
  0.0 168.7 jit_solution(13844385451105794318)
XLA Ops:
  6.5 0.7 all-gather.2.cloned.1.call-update
  7.3 0.2 copy-done
  7.6 0.3 copy-done.1
  7.9 0.3 convolution_convert_fusion
  8.3 4.9 %collective-permute-start.2 = (bf16[8,64,128]{2,1,0:T(8,128)(2,1)S(1)}, bf16[8,64,128]{2,1,0:T(8,128)(2,1)S(1)}, u32[]{:S(2)}, u32[]{:S(2)}) collective-permute-start(bf16[8,64,128]{2,1,0:T(8,128)(2,1)S(1)} %get-tuple-element.7), channel_id=1, source_target_pairs={{0,2},{2,4},{4,6},{6,8},{8,10},{10,12},{12,14},{14,16},{16,18},{18... | collective-permute-start | bytes 393224 | tf_op jit(solution)/shard_map/ppermute | solution.py:17
  13.2 1.3 collective-permute-start.3
  14.5 1.1 fusion.33
  15.5 5.4 %collective-permute-start = (bf16[2048,128]{1,0:T(8,128)(2,1)}, bf16[2048,128]{1,0:T(8,128)(2,1)}, u32[]{:S(2)}, u32[]{:S(2)}) collective-permute-start(bf16[2048,128]{1,0:T(8,128)(2,1)} %get-tuple-element.5), channel_id=1, source_target_pairs={{0,2},{2,4},{4,6},{6,8},{8,10},{10,12},{12,14},{14,16},{16,18},{18... | collective-permute-start | bytes 1572872 | tf_op jit(solution)/shard_map/ppermute | solution.py:17
  20.9 1.3 collective-permute-start.1
  22.7 57.8 %all_gather.11 = bf16[32,64,128]{2,1,0:T(8,128)(2,1)S(1)} all-gather(bf16[2,64,128]{2,1,0:T(8,128)(2,1)S(1)} %fusion.12), channel_id=1, replica_groups=mesh['leaf'=16,'col'=2] {'leaf'}, dimensions={0}, use_global_device_ids=true | all-gather | bytes 557056 | tf_op jit(solution)/shard_map/all_gather | solution.py:73
  80.5 0.4 convolution_convert_fusion.2
  81.3 38.7 %all_gather.10 = bf16[32,64,128]{2,1,0:T(8,128)(2,1)S(1)} all-gather(bf16[2,64,128]{2,1,0:T(8,128)(2,1)S(1)} %bitcast.59), channel_id=1, replica_groups=mesh['leaf'=16,'col'=2] {'leaf'}, dimensions={0}, use_global_device_ids=true | all-gather | bytes 557056 | tf_op jit(solution)/shard_map/all_gather | solution.py:72
  119.9 0.4 convolution_convert_fusion.1
  120.4 0.6 gather_fusion.2
  121.1 0.4 fusion.11
  121.5 0.4 convolution_bitcast_fusion.1
  122.3 1.0 pad_maximum_fusion.1
  123.3 0.7 gather_fusion.1
  124.0 1.9 %fusion.9 = f32[16,128,256]{2,1,0:T(8,128)} fusion(bf16[16,64,256]{2,1,0:T(8,128)(2,1)S(1)} %copy-done, f32[16,64,128]{2,1,0:T(8,128)S(1)} %bitcast.57, bf16[16,64,256]{2,1,0:T(8,128)(2,1)S(1)} %copy-done.3, bf16[16,256,128]{2,1,0:T(8,128)(2,1)S(1)} %bitcast.56), kind=kOutput, calls=%fused_computation.15 | convolution fusion | flops 134479872 | bytes 4718592 | tf_op jit(solution)/shard_map/lrk,lrc->lkc/dot_general | solution.py:105
  126.0 1.7 pad_maximum_fusion
  127.6 6.6 %gather_fusion = bf16[128,256,128]{2,1,0:T(8,128)(2,1)} fusion(bf16[32,256,128]{2,1,0:T(8,128)(2,1)S(1)} %bitcast.52, s32[1024]{0:T(1024)S(1)} %pad_clamp_fusion.2), kind=kCustom, calls=%fused_computation | custom fusion | bytes 16777728 | tf_op jit(solution)/shard_map/gather | solution.py:53
  134.2 12.1 %copy.26 = bf16[128,256,128]{1,2,0:T(8,128)(2,1)} copy(bf16[128,256,128]{2,1,0:T(8,128)(2,1)} %gather_fusion) | data formatting | bytes 16777216 | tf_op jit(solution)/shard_map/gather | solution.py:53
  146.3 12.7 %fusion.4 = f32[16,256,128]{1,2,0:T(8,128)} fusion(f32[16,128,256]{2,1,0:T(8,128)S(1)} %copy-done.2, bf16[16,8,256,256]{3,2,1,0:T(8,128)(2,1)} %all-gather.2.cloned.1.call-done, bf16[16,8,256,128]{2,3,1,0:T(8,128)(2,1)} %bitcast.54, pred[16,8]{1,0:T(8,128)(4,1)S(1)} %iota_compare_fusion), kind=kOutput, calls=%fused_computation.9 | convolution fusion | flops 2152202240 | bytes 29360256 | tf_op jit(solution)/shard_map/lsij,lsjc->lic/dot_general | solution.py:56
  159.0 2.9 %copy.34 = f32[16,256,128]{2,1,0:T(8,128)} copy(f32[16,256,128]{1,2,0:T(8,128)} %fusion.4) | data formatting | bytes 4194304 | tf_op jit(solution)/shard_map/add | solution.py:108
  (51 shorter events, 1.4 us)
Async XLA Ops:
  6.5 1.0 copy-start
  6.5 1.4 copy-start.1
  6.5 139.8 %all-gather.2.cloned.1.call-start = ((), (), s32[]{:S(2)}) async-start(), calls=%async_computation | async-start | bytes 25165824 | tf_op jit(solution)/shard_map/all_gather | solution.py:50
  7.3 14.9 %copy-start.9 = (s32[16,4]{0,1:T(4,128)S(1)}, s32[16,4]{0,1:T(4,128)}, u32[]{:S(2)}) copy-start(s32[16,4]{0,1:T(4,128)} %param.18) | copy-start | bytes 772
  7.3 15.1 %copy-start.4 = (bf16[2,64,512]{2,1,0:T(8,128)(2,1)S(1)}, bf16[2,64,512]{2,1,0:T(8,128)(2,1)}, u32[]{:S(2)}) copy-start(bf16[2,64,512]{2,1,0:T(8,128)(2,1)} %param.19) | copy-start | bytes 393220
  7.3 15.3 %copy-start.6 = (bf16[2,64,64]{2,1,0:T(8,128)(2,1)S(1)}, bf16[2,64,64]{2,1,0:T(8,128)(2,1)}, u32[]{:S(2)}) copy-start(bf16[2,64,64]{2,1,0:T(8,128)(2,1)} %param.22) | copy-start | bytes 49156
  7.3 73.9 %copy-start.11 = (s32[2,4]{1,0:T(2,128)S(1)}, s32[2,4]{1,0:T(2,128)}, u32[]{:S(2)}) copy-start(s32[2,4]{1,0:T(2,128)} %param.21) | copy-start | bytes 100
  7.3 113.1 %copy-start.7 = (bf16[4,64,256]{2,1,0:T(8,128)(2,1)S(1)}, bf16[4,64,256]{2,1,0:T(8,128)(2,1)}, u32[]{:S(2)}) copy-start(bf16[4,64,256]{2,1,0:T(8,128)(2,1)} %param.23) | copy-start | bytes 393220
  7.3 113.7 %copy-start.10 = (s32[16]{0:T(128)S(1)}, s32[16]{0:T(128)}, u32[]{:S(2)}) copy-start(s32[16]{0:T(128)} %param.15) | copy-start | bytes 196
  7.3 113.7 %copy-start.8 = (s32[16,8]{0,1:T(8,128)S(1)}, s32[16,8]{0,1:T(8,128)}, u32[]{:S(2)}) copy-start(s32[16,8]{0,1:T(8,128)} %param.14) | copy-start | bytes 1540
  7.3 114.1 %copy-start.5 = (bf16[2,64,256]{2,1,0:T(8,128)(2,1)S(1)}, bf16[2,64,256]{2,1,0:T(8,128)(2,1)}, u32[]{:S(2)}) copy-start(bf16[2,64,256]{2,1,0:T(8,128)(2,1)} %param.20) | copy-start | bytes 196612
  8.3 114.0 %collective-permute-start.2 = (bf16[8,64,128]{2,1,0:T(8,128)(2,1)S(1)}, bf16[8,64,128]{2,1,0:T(8,128)(2,1)S(1)}, u32[]{:S(2)}, u32[]{:S(2)}) collective-permute-start(bf16[8,64,128]{2,1,0:T(8,128)(2,1)S(1)} %get-tuple-element.7), channel_id=1, source_target_pairs={{0,2},{2,4},{4,6},{6,8},{8,10},{10,12},{12,14},{14,16},{16,18},{18... | collective-permute-start | bytes 393224 | tf_op jit(solution)/shard_map/ppermute | solution.py:17
  13.2 109.1 %collective-permute-start.3 = (bf16[8,64,128]{2,1,0:T(8,128)(2,1)S(1)}, bf16[8,64,128]{2,1,0:T(8,128)(2,1)}, u32[]{:S(2)}, u32[]{:S(2)}) collective-permute-start(bf16[8,64,128]{2,1,0:T(8,128)(2,1)S(1)} %get-tuple-element.8), channel_id=1, source_target_pairs={{2,0},{4,2},{6,4},{8,6},{10,8},{12,10},{14,12},{16,14},{18,16},{20... | collective-permute-start | bytes 393224 | tf_op jit(solution)/shard_map/ppermute | solution.py:18
  15.5 110.4 %collective-permute-start = (bf16[2048,128]{1,0:T(8,128)(2,1)}, bf16[2048,128]{1,0:T(8,128)(2,1)}, u32[]{:S(2)}, u32[]{:S(2)}) collective-permute-start(bf16[2048,128]{1,0:T(8,128)(2,1)} %get-tuple-element.5), channel_id=1, source_target_pairs={{0,2},{2,4},{4,6},{6,8},{8,10},{10,12},{12,14},{14,16},{16,18},{18... | collective-permute-start | bytes 1572872 | tf_op jit(solution)/shard_map/ppermute | solution.py:17
  20.9 105.1 %collective-permute-start.1 = (bf16[2048,128]{1,0:T(8,128)(2,1)}, bf16[2048,128]{1,0:T(8,128)(2,1)}, u32[]{:S(2)}, u32[]{:S(2)}) collective-permute-start(bf16[2048,128]{1,0:T(8,128)(2,1)} %get-tuple-element.6), channel_id=1, source_target_pairs={{2,0},{4,2},{6,4},{8,6},{10,8},{12,10},{14,12},{16,14},{18,16},{20... | collective-permute-start | bytes 1572872 | tf_op jit(solution)/shard_map/ppermute | solution.py:18
  22.7 101.3 %copy-start.3 = (bf16[16,64,256]{2,1,0:T(8,128)(2,1)S(1)}, bf16[16,64,256]{2,1,0:T(8,128)(2,1)}, u32[]{:S(2)}) copy-start(bf16[16,64,256]{2,1,0:T(8,128)(2,1)} %param.17) | copy-start | bytes 1572868
  134.2 12.1 %copy-start.2 = (f32[16,128,256]{2,1,0:T(8,128)S(1)}, f32[16,128,256]{2,1,0:T(8,128)}, u32[]{:S(2)}) copy-start(f32[16,128,256]{2,1,0:T(8,128)} %fusion.9) | copy-start | bytes 6291460
Sparse Core Ops, SparseCore 0:
  8.9 32.7 all-gather.1
where the time goes:
time: 169 us
  blocking collectives  96.5 us (57%)
  local copies, waits for them, and re-layouts  25.4 us (15%)
  matrix products  16.8 us (10%)
  between operations  13.7 us (8%)
  starting transfers between devices  12.8 us (8%)
  other arithmetic  2.82 us (2%)
    all_gather x1, blocking collectives, shards(): lift_piece = lax.all_gather(mid_lift, 'leaf', axis=0, tiled=True)  57.8 us
    all_gather x1, blocking collectives, shards(): coef_piece = lax.all_gather(mid_coef, 'leaf', axis=0, tiled=True)  38.7 us
    gather x2, local copies, waits for them, and re-layouts, shards(): picked = blocks[near_local]  18.7 us
    dot_general x1, matrix products, shards(): jnp.einsum('lsij,lsjc->lic', all_tiles, picked, preferred_element_type=f32)  12.7 us
    ppermute x2, starting transfers between devices, padded(): before = lax.ppermute(last, axis, up)  10.2 us
  transfers between devices with their start and end apart: 5, of which 0 were waited for; matrix products, arithmetic and copies ran while one was open for 17% of the time, Pallas kernels for 0%

commit v1 on v0

--- a/solution.py
+++ b/solution.py
@@ -5,6 +5,18 @@
 
 CHILD = 8
 FAR = 4
+
+
+def gather_by_bits(array, axis, dim):
+    ways, here, step = (lax.axis_size(axis), lax.axis_index(axis), array.shape[dim])
+    line, have = (array, 1)
+    while have < ways:
+        line = jnp.concatenate(
+            [line, lax.ppermute(line, axis, [(d, (d - have) % ways) for d in range(ways)])],
+            axis=dim,
+        )
+        have = 2 * have
+    return jnp.roll(line, here * step, axis=dim)
 
 
 def padded(x, sides, width):
@@ -70,7 +82,7 @@
     mid_flat = mid_far.reshape(-1)
     top_range = jnp.arange(total_top)
     coef_piece = lax.all_gather(mid_coef, "leaf", axis=0, tiled=True)
-    lift_piece = lax.all_gather(mid_lift, "leaf", axis=0, tiled=True)
+    lift_piece = gather_by_bits(mid_lift, "leaf", 0)
     global_ids = jnp.arange(coef_piece.shape[0])
     group_map = (top_range[:, None] == (global_ids // CHILD)[None, :]).astype(bf16)
     top_total = jnp.einsum("pk,krc->prc", group_map, lift_piece, preferred_element_type=f32)

time: 169 us -> 158 us (0.935)
  blocking collectives: 96.5 us -> 54.9 us
  waiting for transfers between devices: 0.72 us -> 14.5 us
  local copies, waits for them, and re-layouts: 25.4 us -> 33.7 us
  starting transfers between devices: 12.8 us -> 16.3 us
  matrix products: 16.8 us -> 19.7 us
    all_gather x1 -> x0, blocking collectives: 57.8 us -> none  [shards(): lift_piece = lax.all_gather(mid_lift, 'leaf', axis=0, tiled=True)]
    all_gather x1, blocking collectives: 38.7 us -> 54.9 us  [shards(): coef_piece = lax.all_gather(mid_coef, 'leaf', axis=0, tiled=True)]
    ppermute x0 -> x4, waiting for transfers between devices: none -> 13.8 us  [gather_by_bits(): lax.ppermute(line, axis, [(d, (d - have) % ways) for d in range(ways)])]
    ppermute x0 -> x4, starting transfers between devices: none -> 7.08 us  [gather_by_bits(): lax.ppermute(line, axis, [(d, (d - have) % ways) for d in range(ways)])]
    unnamed x24 -> x34, local copies, waits for them, and re-layouts: 0.63 us -> 5.82 us
    ppermute x2, starting transfers between devices: 10.2 us -> 6.63 us  [padded(): before = lax.ppermute(last, axis, up)]
  transfers between devices with their start and end apart: 5 -> 9, of which waited for: 0 -> 3; matrix products, arithmetic and copies ran while one was open for 17% -> 26% of each run, Pallas kernels for 0% -> 0%
where the time goes in v1:
time: 158 us; the launch traced here: 157 us
  blocking collectives  54.9 us (35%)
  local copies, waits for them, and re-layouts  33.7 us (21%)
  matrix products  19.7 us (12%)
  starting transfers between devices  16.3 us (10%)
  waiting for transfers between devices  14.5 us (9%)
  between operations  13.7 us (9%)
  other arithmetic  4.17 us (3%)
    all_gather x1, blocking collectives, shards(): coef_piece = lax.all_gather(mid_coef, 'leaf', axis=0, tiled=True)  54.9 us
    gather x2, local copies, waits for them, and re-layouts, shards(): picked = blocks[near_local]  18.7 us
    ppermute x4, waiting for transfers between devices, gather_by_bits(): lax.ppermute(line, axis, [(d, (d - have) % ways) for d in range(ways)])  13.8 us
    dot_general x1, matrix products, shards(): jnp.einsum('lsij,lsjc->lic', all_tiles, picked, preferred_element_type=f32)  12.7 us
    ppermute x4, starting transfers between devices, gather_by_bits(): lax.ppermute(line, axis, [(d, (d - have) % ways) for d in range(ways)])  7.08 us
    ppermute x2, starting transfers between devices, padded(): before = lax.ppermute(last, axis, up)  6.63 us
    unnamed x34, local copies, waits for them, and re-layouts  5.82 us
  transfers between devices with their start and end apart: 9, of which 3 were waited for; matrix products, arithmetic and copies ran while one was open for 26% of the time, Pallas kernels for 0%

profile of v1, /device:TPU:0, one launch (start us, length us, event | category | flops | bytes accessed | tf_op | source)
XLA Modules:
  0.0 157.0 jit_solution(36829596399399992)
XLA Ops:
  8.4 0.7 constant_dynamic-update-slice_fusion.9
  9.2 7.0 %collective-permute-start.4 = (bf16[2,64,128]{2,1,0:T(8,128)(2,1)S(1)}, bf16[2,64,128]{2,1,0:T(8,128)(2,1)S(1)}, u32[]{:S(2)}, u32[]{:S(2)}) collective-permute-start(bf16[2,64,128]{2,1,0:T(8,128)(2,1)S(1)} %get-tuple-element.10), channel_id=1, source_target_pairs={{0,30},{2,0},{4,2},{6,4},{8,6},{10,8},{12,10},{14,12},{16,14},{18,... | collective-permute-start | bytes 98312 | tf_op jit(solution)/shard_map/ppermute | solution.py:15
  16.2 1.3 collective-permute-start.2
  17.5 1.3 collective-permute-start.3
  18.8 1.1 fusion.33
  19.9 5.3 %collective-permute-start = (bf16[2048,128]{1,0:T(8,128)(2,1)}, bf16[2048,128]{1,0:T(8,128)(2,1)}, u32[]{:S(2)}, u32[]{:S(2)}) collective-permute-start(bf16[2048,128]{1,0:T(8,128)(2,1)} %get-tuple-element.5), channel_id=1, source_target_pairs={{0,2},{2,4},{4,6},{6,8},{8,10},{10,12},{12,14},{14,16},{16,18},{18... | collective-permute-start | bytes 1572872 | tf_op jit(solution)/shard_map/ppermute | solution.py:29
  25.2 1.3 collective-permute-start.1
  27.0 54.9 %all_gather.7 = bf16[32,64,128]{2,1,0:T(8,128)(2,1)S(1)} all-gather(bf16[2,64,128]{2,1,0:T(8,128)(2,1)S(1)} %bitcast.59), channel_id=1, replica_groups=mesh['leaf'=16,'col'=2] {'leaf'}, dimensions={0}, use_global_device_ids=true | all-gather | bytes 557056 | tf_op jit(solution)/shard_map/all_gather | solution.py:84
  82.6 4.2 %collective-permute-done.5 = bf16[4,64,128]{2,1,0:T(8,128)(2,1)S(1)} collective-permute-done((bf16[4,64,128]{2,1,0:T(8,128)(2,1)S(1)}, bf16[4,64,128]{2,1,0:T(8,128)(2,1)S(1)}, u32[]{:S(2)}, u32[]{:S(2)}) %collective-permute-start.5) | collective-permute-done | bytes 65568 | tf_op jit(solution)/shard_map/ppermute | solution.py:15
  88.3 1.2 gather_fusion.2
  90.1 2.5 %collective-permute-done.6 = bf16[8,64,128]{2,1,0:T(8,128)(2,1)S(1)} collective-permute-done((bf16[8,64,128]{2,1,0:T(8,128)(2,1)S(1)}, bf16[8,64,128]{2,1,0:T(8,128)(2,1)S(1)}, u32[]{:S(2)}, u32[]{:S(2)}) %collective-permute-start.6) | collective-permute-done | bytes 131104 | tf_op jit(solution)/shard_map/ppermute | solution.py:15
  94.0 1.0 pad_maximum_fusion.1
  95.0 0.7 gather_fusion.1
  96.4 7.1 %collective-permute-done.7 = bf16[16,64,128]{2,1,0:T(8,128)(2,1)S(1)} collective-permute-done((bf16[16,64,128]{2,1,0:T(8,128)(2,1)}, bf16[16,64,128]{2,1,0:T(8,128)(2,1)S(1)}, u32[]{:S(2)}, u32[]{:S(2)}) %collective-permute-start.7) | collective-permute-done | bytes 262176 | tf_op jit(solution)/shard_map/ppermute | solution.py:15
  107.5 1.1 constant_dynamic-slice_fusion
  108.6 1.1 convolution_convert_fusion.2
  109.7 1.2 fusion.11
  110.8 1.2 convolution_bitcast_fusion.1
  112.3 1.9 %fusion.9 = f32[16,128,256]{2,1,0:T(8,128)} fusion(bf16[16,64,256]{2,1,0:T(8,128)(2,1)S(1)} %copy-done, f32[16,64,128]{2,1,0:T(8,128)S(1)} %bitcast.57, bf16[16,64,256]{2,1,0:T(8,128)(2,1)S(1)} %copy-done.3, bf16[16,256,128]{2,1,0:T(8,128)(2,1)S(1)} %bitcast.56), kind=kOutput, calls=%fused_computation.15 | convolution fusion | flops 134479872 | bytes 4718592 | tf_op jit(solution)/shard_map/lrk,lrc->lkc/dot_general | solution.py:117
  114.2 1.7 %pad_maximum_fusion = bf16[8192,128]{1,0:T(8,128)(2,1)S(1)} fusion(bf16[2048,128]{1,0:T(8,128)(2,1)} %collective-permute-done.1, bf16[4096,128]{1,0:T(8,128)(2,1)} %param.12, bf16[2048,128]{1,0:T(8,128)(2,1)} %collective-permute-done), kind=kLoop, calls=%fused_computation.7 | loop fusion | flops 6291456 | bytes 4194304 | tf_op jit(solution)/shard_map/concatenate | solution.py:31
  115.9 6.6 %gather_fusion = bf16[128,256,128]{2,1,0:T(8,128)(2,1)} fusion(bf16[32,256,128]{2,1,0:T(8,128)(2,1)S(1)} %bitcast.52, s32[1024]{0:T(1024)S(1)} %pad_clamp_fusion.2), kind=kCustom, calls=%fused_computation | custom fusion | bytes 16777728 | tf_op jit(solution)/shard_map/gather | solution.py:65
  122.5 12.1 %copy.28 = bf16[128,256,128]{1,2,0:T(8,128)(2,1)} copy(bf16[128,256,128]{2,1,0:T(8,128)(2,1)} %gather_fusion) | data formatting | bytes 16777216 | tf_op jit(solution)/shard_map/gather | solution.py:65
  134.6 12.7 %fusion.4 = f32[16,256,128]{1,2,0:T(8,128)} fusion(f32[16,128,256]{2,1,0:T(8,128)S(1)} %copy-done.2, bf16[16,8,256,256]{3,2,1,0:T(8,128)(2,1)} %all-gather.2.cloned.1.call-done, bf16[16,8,256,128]{2,3,1,0:T(8,128)(2,1)} %bitcast.54, pred[16,8]{1,0:T(8,128)(4,1)S(1)} %iota_compare_fusion), kind=kOutput, calls=%fused_computation.9 | convolution fusion | flops 2152202240 | bytes 29360256 | tf_op jit(solution)/shard_map/lsij,lsjc->lic/dot_general | solution.py:68
  147.3 2.9 %copy.36 = f32[16,256,128]{2,1,0:T(8,128)} copy(f32[16,256,128]{1,2,0:T(8,128)} %fusion.4) | data formatting | bytes 4194304 | tf_op jit(solution)/shard_map/add | solution.py:120
  (73 shorter events, 11.3 us)
Async XLA Ops:
  6.5 1.0 copy-start
  6.5 1.4 copy-start.1
  6.5 1.7 %copy-start.4 = (bf16[2,64,512]{2,1,0:T(8,128)(2,1)S(1)}, bf16[2,64,512]{2,1,0:T(8,128)(2,1)}, u32[]{:S(2)}) copy-start(bf16[2,64,512]{2,1,0:T(8,128)(2,1)} %param.19) | copy-start | bytes 393220
  6.5 1.9 %copy-start.8 = (bf16[2,64,64]{2,1,0:T(8,128)(2,1)S(1)}, bf16[2,64,64]{2,1,0:T(8,128)(2,1)}, u32[]{:S(2)}) copy-start(bf16[2,64,64]{2,1,0:T(8,128)(2,1)} %param.22) | copy-start | bytes 49156
  6.5 128.1 %all-gather.2.cloned.1.call-start = ((), (), s32[]{:S(2)}) async-start(), calls=%async_computation | async-start | bytes 25165824 | tf_op jit(solution)/shard_map/all_gather | solution.py:62
  7.3 19.2 %copy-start.12 = (s32[2,4]{1,0:T(2,128)S(1)}, s32[2,4]{1,0:T(2,128)}, u32[]{:S(2)}) copy-start(s32[2,4]{1,0:T(2,128)} %param.21) | copy-start | bytes 100
  7.3 19.3 %copy-start.10 = (s32[16,4]{0,1:T(4,128)S(1)}, s32[16,4]{0,1:T(4,128)}, u32[]{:S(2)}) copy-start(s32[16,4]{0,1:T(4,128)} %param.18) | copy-start | bytes 772
  7.3 19.6 %copy-start.11 = (s32[16]{0:T(128)S(1)}, s32[16]{0:T(128)}, u32[]{:S(2)}) copy-start(s32[16]{0:T(128)} %param.15) | copy-start | bytes 196
  7.3 19.7 %copy-start.9 = (s32[16,8]{0,1:T(8,128)S(1)}, s32[16,8]{0,1:T(8,128)}, u32[]{:S(2)}) copy-start(s32[16,8]{0,1:T(8,128)} %param.14) | copy-start | bytes 1540
  7.3 81.0 %copy-start.7 = (bf16[4,64,256]{2,1,0:T(8,128)(2,1)S(1)}, bf16[4,64,256]{2,1,0:T(8,128)(2,1)}, u32[]{:S(2)}) copy-start(bf16[4,64,256]{2,1,0:T(8,128)(2,1)} %param.23) | copy-start | bytes 393220
  9.2 73.3 %collective-permute-start.4 = (bf16[2,64,128]{2,1,0:T(8,128)(2,1)S(1)}, bf16[2,64,128]{2,1,0:T(8,128)(2,1)S(1)}, u32[]{:S(2)}, u32[]{:S(2)}) collective-permute-start(bf16[2,64,128]{2,1,0:T(8,128)(2,1)S(1)} %get-tuple-element.10), channel_id=1, source_target_pairs={{0,30},{2,0},{4,2},{6,4},{8,6},{10,8},{12,10},{14,12},{16,14},{18,... | collective-permute-start | bytes 98312 | tf_op jit(solution)/shard_map/ppermute | solution.py:15
  16.2 77.8 %collective-permute-start.2 = (bf16[8,64,128]{2,1,0:T(8,128)(2,1)S(1)}, bf16[8,64,128]{2,1,0:T(8,128)(2,1)S(1)}, u32[]{:S(2)}, u32[]{:S(2)}) collective-permute-start(bf16[8,64,128]{2,1,0:T(8,128)(2,1)S(1)} %get-tuple-element.7), channel_id=1, source_target_pairs={{0,2},{2,4},{4,6},{6,8},{8,10},{10,12},{12,14},{14,16},{16,18},{18... | collective-permute-start | bytes 393224 | tf_op jit(solution)/shard_map/ppermute | solution.py:29
  17.5 76.5 %collective-permute-start.3 = (bf16[8,64,128]{2,1,0:T(8,128)(2,1)S(1)}, bf16[8,64,128]{2,1,0:T(8,128)(2,1)}, u32[]{:S(2)}, u32[]{:S(2)}) collective-permute-start(bf16[8,64,128]{2,1,0:T(8,128)(2,1)S(1)} %get-tuple-element.8), channel_id=1, source_target_pairs={{2,0},{4,2},{6,4},{8,6},{10,8},{12,10},{14,12},{16,14},{18,16},{20... | collective-permute-start | bytes 393224 | tf_op jit(solution)/shard_map/ppermute | solution.py:30
  19.9 94.4 %collective-permute-start = (bf16[2048,128]{1,0:T(8,128)(2,1)}, bf16[2048,128]{1,0:T(8,128)(2,1)}, u32[]{:S(2)}, u32[]{:S(2)}) collective-permute-start(bf16[2048,128]{1,0:T(8,128)(2,1)} %get-tuple-element.5), channel_id=1, source_target_pairs={{0,2},{2,4},{4,6},{6,8},{8,10},{10,12},{12,14},{14,16},{16,18},{18... | collective-permute-start | bytes 1572872 | tf_op jit(solution)/shard_map/ppermute | solution.py:29
  25.2 89.0 %collective-permute-start.1 = (bf16[2048,128]{1,0:T(8,128)(2,1)}, bf16[2048,128]{1,0:T(8,128)(2,1)}, u32[]{:S(2)}, u32[]{:S(2)}) collective-permute-start(bf16[2048,128]{1,0:T(8,128)(2,1)} %get-tuple-element.6), channel_id=1, source_target_pairs={{2,0},{4,2},{6,4},{8,6},{10,8},{12,10},{14,12},{16,14},{18,16},{20... | collective-permute-start | bytes 1572872 | tf_op jit(solution)/shard_map/ppermute | solution.py:30
  82.5 4.3 %collective-permute-start.5 = (bf16[4,64,128]{2,1,0:T(8,128)(2,1)S(1)}, bf16[4,64,128]{2,1,0:T(8,128)(2,1)S(1)}, u32[]{:S(2)}, u32[]{:S(2)}) collective-permute-start(bf16[4,64,128]{2,1,0:T(8,128)(2,1)S(1)} %pad_maximum_fusion.4), channel_id=1, source_target_pairs={{0,28},{2,30},{4,0},{6,2},{8,4},{10,6},{12,8},{14,10},{16,12},{18,... | collective-permute-start | bytes 196616 | tf_op jit(solution)/shard_map/ppermute | solution.py:15
  86.8 5.7 %collective-permute-start.6 = (bf16[8,64,128]{2,1,0:T(8,128)(2,1)S(1)}, bf16[8,64,128]{2,1,0:T(8,128)(2,1)S(1)}, u32[]{:S(2)}, u32[]{:S(2)}) collective-permute-start(bf16[8,64,128]{2,1,0:T(8,128)(2,1)S(1)} %pad_maximum_fusion.3), channel_id=1, source_target_pairs={{0,24},{2,26},{4,28},{6,30},{8,0},{10,2},{12,4},{14,6},{16,8},{18,... | collective-permute-start | bytes 393224 | tf_op jit(solution)/shard_map/ppermute | solution.py:15
  93.3 10.2 %collective-permute-start.7 = (bf16[16,64,128]{2,1,0:T(8,128)(2,1)}, bf16[16,64,128]{2,1,0:T(8,128)(2,1)S(1)}, u32[]{:S(2)}, u32[]{:S(2)}) collective-permute-start(bf16[16,64,128]{2,1,0:T(8,128)(2,1)} %pad_maximum_fusion.2), channel_id=1, source_target_pairs={{0,16},{2,18},{4,20},{6,22},{8,24},{10,26},{12,28},{14,30},{16,0},... | collective-permute-start | bytes 786440 | tf_op jit(solution)/shard_map/ppermute | solution.py:15
  94.9 14.7 %copy-start.6 = (bf16[2,64,256]{2,1,0:T(8,128)(2,1)S(1)}, bf16[2,64,256]{2,1,0:T(8,128)(2,1)}, u32[]{:S(2)}) copy-start(bf16[2,64,256]{2,1,0:T(8,128)(2,1)} %gather_fusion.2) | copy-start | bytes 196612
  95.0 15.9 %copy-start.5 = (bf16[8,64,128]{2,1,0:T(8,128)(2,1)S(1)}, bf16[8,64,128]{2,1,0:T(8,128)(2,1)}, u32[]{:S(2)}) copy-start(bf16[8,64,128]{2,1,0:T(8,128)(2,1)} %copy.31) | copy-start | bytes 393220
  95.0 17.3 %copy-start.3 = (bf16[16,64,256]{2,1,0:T(8,128)(2,1)S(1)}, bf16[16,64,256]{2,1,0:T(8,128)(2,1)}, u32[]{:S(2)}) copy-start(bf16[16,64,256]{2,1,0:T(8,128)(2,1)} %param.17) | copy-start | bytes 1572868
  122.5 12.2 %copy-start.2 = (f32[16,128,256]{2,1,0:T(8,128)S(1)}, f32[16,128,256]{2,1,0:T(8,128)}, u32[]{:S(2)}) copy-start(f32[16,128,256]{2,1,0:T(8,128)} %fusion.9) | copy-start | bytes 6291460
Sparse Core Ops, SparseCore 0:
  8.9 32.7 all-gather.1
